TPU v7x, 256 devices: a whole 4x4x8 slice. The times are simulated.
256 devices in a mesh: src: 32 (over z, y), tgt: 8 (over x, core).
Axes of the slice: x: 4, y: 4, z: 8, core: 2. Of those that a mesh axis runs over, the one named last changes fastest.
Arguments:
- source: bfloat16 [32768, 300], P('src'), may hold values from -70 to 70
- target: bfloat16 [16384, 300], P('tgt'), may hold values from -11 to 11
- start_map: float32 [300, 300], replicated, may hold values from -1.5 to 1.5
Outputs:
- source_soft: bfloat16 [32768, 300], P(('src', 'tgt'))
- target_soft: bfloat16 [16384, 300], P('tgt')
- polar_map: float32 [300, 300], replicated
All inputs are finite; a program needn't handle non-finite values.
Results may differ from a plain program's by a relative error of at most 0.014.
The roundings to bfloat16 on the way count: a program that leaves them out, or rounds other values in their place, can miss the bound.
Values may be sent and summed in bfloat16 or wider, within the bound.
A program may use at most 64 MiB of HBM per device.

v0:
```python
import math
import jax
import jax.numpy as jnp
from jax import lax
from jax.sharding import PartitionSpec as P

ITERS = 2
NEWTON_STEPS = 8


def polar_steps(covariance):
    highest = lax.Precision.HIGHEST
    current = covariance / jnp.sqrt(jnp.sum(covariance * covariance) + 1e-06)
    for newton in range(NEWTON_STEPS):
        gram_matrix = jnp.dot(current.T, current, precision=highest)
        current = 1.5 * current - 0.5 * jnp.dot(current, gram_matrix, precision=highest)
    return current


def merge_stats(top, total, axis):
    gathered = lax.all_gather(jnp.stack([top, total]), axis)
    tops, totals = (gathered[:, 0], gathered[:, 1])
    best = jnp.max(tops, axis=0)
    return (best, jnp.sum(totals * jnp.exp(tops - best[None]), axis=0))


def body(source, target, start_map):
    highest = lax.Precision.HIGHEST
    score_scale = 2.0 / math.sqrt(source.shape[1])
    source_f32 = source.astype(jnp.float32)
    target_f32 = target.astype(jnp.float32)
    current = start_map
    for iteration in range(ITERS):
        mapped = jnp.dot(
            source, current.astype(jnp.bfloat16), preferred_element_type=jnp.float32
        ).astype(jnp.bfloat16)
        scores = (
            lax.dot_general(
                mapped, target, (((1,), (1,)), ((), ())), preferred_element_type=jnp.float32
            )
            * score_scale
        )
        row_local = jnp.max(scores, axis=1)
        col_local = jnp.max(scores, axis=0)
        row_part = jnp.sum(jnp.exp(scores - row_local[:, None]), axis=1)
        col_part = jnp.sum(jnp.exp(scores - col_local[None, :]), axis=0)
        row_top, row_total = merge_stats(row_local, row_part, "tgt")
        col_top, col_total = merge_stats(col_local, col_part, "src")
        row_weights = (jnp.exp(scores - row_top[:, None]) / row_total[:, None]).astype(jnp.bfloat16)
        col_weights = (jnp.exp(scores - col_top[None, :]) / col_total[None, :]).astype(jnp.bfloat16)
        source_part = jnp.dot(row_weights, target, preferred_element_type=jnp.float32)
        target_part = lax.dot_general(
            col_weights, source, (((0,), (0,)), ((), ())), preferred_element_type=jnp.float32
        )
        covariance = jnp.dot(source_f32.T, source_part, precision=highest)
        covariance = covariance + jnp.dot(target_part.T, target_f32, precision=highest)
        covariance = lax.psum(covariance, ("src", "tgt"))
        if iteration == ITERS - 1:
            source_soft = lax.psum_scatter(
                source_part, "tgt", scatter_dimension=0, tiled=True
            ).astype(jnp.bfloat16)
            target_soft = lax.psum(target_part, "src").astype(jnp.bfloat16)
        current = polar_steps(covariance)
    return (source_soft, target_soft, current)


def solution(mesh):
    in_specs = (P("src", None), P("tgt", None), P())
    out_specs = (P(("src", "tgt"), None), P("tgt", None), P())
    return jax.shard_map(body, mesh=mesh, in_specs=in_specs, out_specs=out_specs, check_vma=False)
```

profile of v0, /device:TPU:8, one launch (start us, length us, event | category | flops | bytes accessed | tf_op | source)
XLA Modules:
  0.0 762.6 jit_solution(12833689186775290613)
XLA Ops:
  8.5 7.3 multiply_reduce_fusion.3
  15.8 5.1 exponential_reduce_fusion.3
  21.6 1.4 exponential_reduce_fusion.2
  23.0 52.3 %all-gather.5 = f32[32,2,2048]{2,1,0:T(2,128)S(1)} all-gather(f32[1,2,2048]{2,1,0:T(2,128)S(1)} %maximum_bitcast_fusion), channel_id=3, replica_groups=mesh['src'=32,'tgt'=8] {'src'}, dimensions={0}, use_global_device_ids=true | all-gather | bytes 540672 | tf_op jit(solution)/shard_map/all_gather | solution.py:21
  76.0 2.5 fusion
  78.5 2.2 fusion.46
  80.7 13.3 %all-gather.4 = f32[8,2,1024]{2,1,0:T(2,128)S(1)} all-gather(f32[1,2,1024]{2,1,0:T(2,128)S(1)} %maximum_bitcast_fusion.2), channel_id=2, replica_groups=mesh['src'=32,'tgt'=8] {'tgt'}, dimensions={0}, use_global_device_ids=true | all-gather | bytes 73728 | tf_op jit(solution)/shard_map/all_gather | solution.py:21
  94.1 2.5 fusion.2
  96.7 3.4 fusion.22
  100.2 249.1 %all-reduce.4.cloned.1.call-done = f32[300,300]{0,1:T(8,128)} async-done(((f32[300,300]{0,1:T(8,128)}), f32[300,300]{0,1:T(8,128)}) %all-reduce.4.cloned.1.call-update) | async-done | bytes 360016 | tf_op jit(solution)/shard_map/psum | solution.py:57
  349.3 1.7 multiply_reduce_fusion.5
  351.7 2.2 fusion.32
  353.9 2.4 fusion.21
  359.7 1.3 fusion.19
  365.6 12.7 %fusion.51 = f32[300,300]{1,0:T(8,128)S(1)} fusion(f32[300,300]{0,1:T(8,128)S(1)} %fusion.17), kind=kOutput, calls=%fused_computation.101 | convolution fusion | flops 324000000 | bytes 720000 | tf_op jit(solution)/shard_map/dot_general | solution.py:15
  384.1 5.3 multiply_reduce_fusion
  389.4 6.0 exponential_reduce_fusion
  395.4 12.9 %all-gather.6 = f32[8,2,1024]{2,1,0:T(2,128)S(1)} all-gather(f32[1,2,1024]{2,1,0:T(2,128)S(1)} %maximum_bitcast_fusion.3), channel_id=4, replica_groups=mesh['src'=32,'tgt'=8] {'tgt'}, dimensions={0}, use_global_device_ids=true | all-gather | bytes 73728 | tf_op jit(solution)/shard_map/all_gather | solution.py:21
  408.4 3.2 fusion.3
  412.8 47.7 %all-gather.7 = f32[32,2,2048]{2,1,0:T(2,128)S(1)} all-gather(f32[1,2,2048]{2,1,0:T(2,128)S(1)} %maximum_bitcast_fusion.1), channel_id=5, replica_groups=mesh['src'=32,'tgt'=8] {'src'}, dimensions={0}, use_global_device_ids=true | all-gather | bytes 540672 | tf_op jit(solution)/shard_map/all_gather | solution.py:21
  461.2 4.5 fusion.1
  465.8 1.4 copy-done.2
  467.2 2.9 convolution_add_fusion
  470.2 164.8 %all-reduce.7 = bf16[2048,300]{0,1:T(8,128)(2,1)} all-reduce(f32[2048,300]{0,1:T(8,128)} %copy-done.2), channel_id=1, replica_groups=mesh['src'=32,'tgt'=8] {'src'}, use_global_device_ids=true, to_apply=%region_19.0 | all-reduce | flops 614400 | bytes 3686400 | tf_op jit(solution)/shard_map/psum | solution.py:62
  635.0 84.4 %all-reduce.6.cloned.1.call-done = f32[300,300]{0,1:T(8,128)} async-done(((f32[300,300]{0,1:T(8,128)}), f32[300,300]{0,1:T(8,128)}) %all-reduce.6.cloned.1.call-update) | async-done | bytes 360016 | tf_op jit(solution)/shard_map/psum | solution.py:57
  719.3 1.7 multiply_reduce_fusion.4
  721.8 2.2 fusion.33
  724.0 2.4 fusion.13
  735.6 1.3 fusion.58
  739.2 1.3 fusion.7
  743.7 10.3 %reduce-scatter.2.cloned.1.call-done = f32[128,300]{0,1:T(8,128)} async-done(((f32[1024,300]{0,1:T(8,128)}), f32[128,300]{0,1:T(8,128)}) %reduce-scatter.2.cloned.1.call-update) | async-done | bytes 153616 | tf_op jit(solution)/shard_map/reduce_scatter | solution.py:59
  754.1 1.6 convert_element_type.40
  (55 shorter events, 33.1 us)
Async XLA Ops:
  7.2 1.3 copy-start
  7.2 342.1 %all-reduce.4.cloned.1.call-start = ((), (), s32[]{:S(2)}) async-start(), calls=%async_computation.1 | async-start | bytes 933888 | tf_op jit(solution)/shard_map/psum | solution.py:57
  15.8 5.8 copy-start.1
  15.8 60.2 %copy-start.4 = (bf16[1024,300]{0,1:T(8,128)(2,1)S(1)}, bf16[1024,300]{0,1:T(8,128)(2,1)}, u32[]{:S(2)}) copy-start(bf16[1024,300]{0,1:T(8,128)(2,1)} %param.3) | copy-start | bytes 1843204
  100.1 619.2 %all-reduce.6.cloned.1.call-start = ((), (), s32[]{:S(2)}) async-start(), calls=%async_computation.3 | async-start | bytes 933888 | tf_op jit(solution)/shard_map/psum | solution.py:57
  389.4 19.0 %copy-start.3 = (f32[1024,2048]{1,0:T(8,128)S(1)}, f32[1024,2048]{1,0:T(8,128)}, u32[]{:S(2)}) copy-start(f32[1024,2048]{1,0:T(8,128)} %get-tuple-element.29) | copy-start | bytes 25165828
  411.7 54.1 %copy-start.5 = (f32[1024,300]{0,1:T(8,128)}, f32[1024,300]{0,1:T(8,128)S(1)}, u32[]{:S(2)}) copy-start(f32[1024,300]{0,1:T(8,128)S(1)} %fusion.3) | copy-start | bytes 3686404
  465.8 1.4 copy-start.2
  470.1 283.9 %reduce-scatter.2.cloned.1.call-start = ((), (), s32[]{:S(2)}) async-start(), calls=%async_computation.2 | async-start | bytes 1400832 | tf_op jit(solution)/shard_map/reduce_scatter | solution.py:59
Sparse Core Ops, SparseCore 0:
  100.3 248.9 all-reduce.3
  470.3 249.0 all-reduce.5
  721.9 32.1 reduce-scatter.1
where the time goes:
time: 771 us; the launch traced here: 763 us
  waiting for transfers between devices  344 us (45%)
  blocking collectives  291 us (38%)
  matrix products  88.1 us (11%)
  other arithmetic  19.2 us (2%)
  between operations  16 us (2%)
    psum x2, waiting for transfers between devices, body(): covariance = lax.psum(covariance, ('src', 'tgt'))  333 us
    psum x1, blocking collectives, body(): target_soft = lax.psum(target_part, 'src').astype(jnp.bfloat16)  165 us
    all_gather x4, blocking collectives, merge_stats(): gathered = lax.all_gather(jnp.stack([top, total]), axis)  126 us
    dot_general x16, matrix products, polar_steps(): gram_matrix = jnp.dot(current.T, current, precision=highest)  30.9 us
    dot_general x16, matrix products, polar_steps(): jnp.dot(current, gram_matrix, precision=highest)  22.2 us
  transfers between devices with their start and end apart: 3, of which 3 were waited for; matrix products, arithmetic and copies ran while one was open for 3% of the time, Pallas kernels for 0%

commit v1 on v0

--- a/solution.py
+++ b/solution.py
@@ -54,7 +54,7 @@
         )
         covariance = jnp.dot(source_f32.T, source_part, precision=highest)
         covariance = covariance + jnp.dot(target_part.T, target_f32, precision=highest)
-        covariance = lax.psum(covariance, ("src", "tgt"))
+        covariance = lax.psum(lax.psum(covariance, "tgt"), "src")
         if iteration == ITERS - 1:
             source_soft = lax.psum_scatter(
                 source_part, "tgt", scatter_dimension=0, tiled=True

time: 771 us -> 716 us (0.929)
  waiting for transfers between devices: 344 us -> 286 us
    psum x2 -> x4, waiting for transfers between devices: 333 us -> 276 us  [body(): covariance = lax.psum(lax.psum(covariance, 'tgt'), 'src')]
  transfers between devices with their start and end apart: 3 -> 5, of which waited for: 3 -> 4; matrix products, arithmetic and copies ran while one was open for 3% -> 3% of each run, Pallas kernels for 0% -> 0%
where the time goes in v1:
time: 716 us; the launch traced here: 707 us
  blocking collectives  294 us (41%)
  waiting for transfers between devices  286 us (40%)
  matrix products  88.2 us (12%)
  other arithmetic  19.2 us (3%)
  between operations  16 us (2%)
    psum x4, waiting for transfers between devices, body(): covariance = lax.psum(lax.psum(covariance, 'tgt'), 'src')  276 us
    psum x1, blocking collectives, body(): target_soft = lax.psum(target_part, 'src').astype(jnp.bfloat16)  167 us
    all_gather x4, blocking collectives, merge_stats(): gathered = lax.all_gather(jnp.stack([top, total]), axis)  127 us
    dot_general x16, matrix products, polar_steps(): gram_matrix = jnp.dot(current.T, current, precision=highest)  30.9 us
    dot_general x16, matrix products, polar_steps(): jnp.dot(current, gram_matrix, precision=highest)  22.2 us
  transfers between devices with their start and end apart: 5, of which 4 were waited for; matrix products, arithmetic and copies ran while one was open for 3% of the time, Pallas kernels for 0%

profile of v1, /device:TPU:8, one launch (start us, length us, event | category | flops | bytes accessed | tf_op | source)
XLA Modules:
  0.0 707.4 jit_solution(5602931502422819669)
XLA Ops:
  8.5 7.3 %multiply_reduce_fusion.3 = (f32[1024]{0:T(1024)S(1)}, f32[1024,2048]{1,0:T(8,128)}) fusion(bf16[2048,300]{0,1:T(8,128)(2,1)S(1)} %copy-done, bf16[1024,300]{0,1:T(8,128)(2,1)} %param.3, f32[300,300]{1,0:T(8,128)} %param.5), kind=kOutput, calls=%fused_computation.11 | convolution fusion | flops 1447201664 | bytes 10595904 | tf_op jit(solution)/shard_map/dot_general | solution.py:38
  15.8 5.1 exponential_reduce_fusion.3
  21.6 1.4 exponential_reduce_fusion.2
  23.0 52.3 %all-gather.5 = f32[32,2,2048]{2,1,0:T(2,128)S(1)} all-gather(f32[1,2,2048]{2,1,0:T(2,128)S(1)} %maximum_bitcast_fusion), channel_id=3, replica_groups=mesh['src'=32,'tgt'=8] {'src'}, dimensions={0}, use_global_device_ids=true | all-gather | bytes 540672 | tf_op jit(solution)/shard_map/all_gather | solution.py:21
  76.0 2.5 fusion
  78.5 2.2 fusion.46
  80.7 13.3 %all-gather.4 = f32[8,2,1024]{2,1,0:T(2,128)S(1)} all-gather(f32[1,2,1024]{2,1,0:T(2,128)S(1)} %maximum_bitcast_fusion.2), channel_id=2, replica_groups=mesh['src'=32,'tgt'=8] {'tgt'}, dimensions={0}, use_global_device_ids=true | all-gather | bytes 73728 | tf_op jit(solution)/shard_map/all_gather | solution.py:21
  94.1 2.5 fusion.2
  96.7 3.4 fusion.22
  100.2 63.2 %all-reduce.6.cloned.1.call-done = f32[300,300]{0,1:T(8,128)} async-done(((f32[300,300]{0,1:T(8,128)}), f32[300,300]{0,1:T(8,128)}) %all-reduce.6.cloned.1.call-update) | async-done | bytes 360016 | tf_op jit(solution)/shard_map/psum | solution.py:57
  163.5 148.7 %all-reduce.8.cloned.1.call-done = f32[300,300]{0,1:T(8,128)} async-done(((f32[300,300]{0,1:T(8,128)}), f32[300,300]{0,1:T(8,128)}) %all-reduce.8.cloned.1.call-update) | async-done | bytes 360016 | tf_op jit(solution)/shard_map/psum | solution.py:57
  312.1 1.7 multiply_reduce_fusion.5
  314.6 2.2 fusion.32
  316.8 2.4 fusion.21
  322.6 1.3 fusion.19
  328.4 12.7 %fusion.51 = f32[300,300]{1,0:T(8,128)S(1)} fusion(f32[300,300]{0,1:T(8,128)S(1)} %fusion.17), kind=kOutput, calls=%fused_computation.101 | convolution fusion | flops 324000000 | bytes 720000 | tf_op jit(solution)/shard_map/dot_general | solution.py:15
  347.0 5.3 multiply_reduce_fusion
  352.3 6.0 exponential_reduce_fusion
  358.3 13.1 %all-gather.6 = f32[8,2,1024]{2,1,0:T(2,128)S(1)} all-gather(f32[1,2,1024]{2,1,0:T(2,128)S(1)} %maximum_bitcast_fusion.3), channel_id=4, replica_groups=mesh['src'=32,'tgt'=8] {'tgt'}, dimensions={0}, use_global_device_ids=true | all-gather | bytes 73728 | tf_op jit(solution)/shard_map/all_gather | solution.py:21
  371.5 3.2 fusion.3
  375.9 48.1 %all-gather.7 = f32[32,2,2048]{2,1,0:T(2,128)S(1)} all-gather(f32[1,2,2048]{2,1,0:T(2,128)S(1)} %maximum_bitcast_fusion.1), channel_id=5, replica_groups=mesh['src'=32,'tgt'=8] {'src'}, dimensions={0}, use_global_device_ids=true | all-gather | bytes 540672 | tf_op jit(solution)/shard_map/all_gather | solution.py:21
  424.7 4.5 fusion.1
  429.3 1.4 copy-done.2
  430.7 2.9 convolution_add_fusion
  433.7 63.9 %all-reduce.10.cloned.1.call-done = f32[300,300]{0,1:T(8,128)} async-done(((f32[300,300]{0,1:T(8,128)}), f32[300,300]{0,1:T(8,128)}) %all-reduce.10.cloned.1.call-update) | async-done | bytes 360016 | tf_op jit(solution)/shard_map/psum | solution.py:57
  497.6 166.7 %all-reduce.13 = bf16[2048,300]{0,1:T(8,128)(2,1)} all-reduce(f32[2048,300]{0,1:T(8,128)} %copy-done.2), channel_id=1, replica_groups=mesh['src'=32,'tgt'=8] {'src'}, use_global_device_ids=true, to_apply=%region_20.0 | all-reduce | flops 614400 | bytes 3686400 | tf_op jit(solution)/shard_map/psum | solution.py:62
  664.4 1.7 multiply_reduce_fusion.4
  666.9 2.2 fusion.33
  669.1 2.4 fusion.13
  680.7 1.3 fusion.58
  688.8 10.1 %reduce-scatter.2.cloned.1.call-done = f32[128,300]{0,1:T(8,128)} async-done(((f32[1024,300]{0,1:T(8,128)}), f32[128,300]{0,1:T(8,128)}) %reduce-scatter.2.cloned.1.call-update) | async-done | bytes 153616 | tf_op jit(solution)/shard_map/reduce_scatter | solution.py:59
  698.9 1.6 convert_element_type.40
  (61 shorter events, 34.5 us)
Async XLA Ops:
  7.2 1.3 copy-start
  7.2 156.2 %all-reduce.6.cloned.1.call-start = ((), (), s32[]{:S(2)}) async-start(), calls=%async_computation.1 | async-start | bytes 933888 | tf_op jit(solution)/shard_map/psum | solution.py:57
  15.8 5.8 copy-start.1
  15.8 60.2 %copy-start.4 = (bf16[1024,300]{0,1:T(8,128)(2,1)S(1)}, bf16[1024,300]{0,1:T(8,128)(2,1)}, u32[]{:S(2)}) copy-start(bf16[1024,300]{0,1:T(8,128)(2,1)} %param.3) | copy-start | bytes 1843204
  100.1 212.0 %all-reduce.8.cloned.1.call-start = ((), (), s32[]{:S(2)}) async-start(), calls=%async_computation.2 | async-start | bytes 933888 | tf_op jit(solution)/shard_map/psum | solution.py:57
  163.4 334.2 %all-reduce.10.cloned.1.call-start = ((), (), s32[]{:S(2)}) async-start(), calls=%async_computation.4 | async-start | bytes 933888 | tf_op jit(solution)/shard_map/psum | solution.py:57
  352.3 19.2 %copy-start.3 = (f32[1024,2048]{1,0:T(8,128)S(1)}, f32[1024,2048]{1,0:T(8,128)}, u32[]{:S(2)}) copy-start(f32[1024,2048]{1,0:T(8,128)} %get-tuple-element.29) | copy-start | bytes 25165828
  374.7 54.5 %copy-start.5 = (f32[1024,300]{0,1:T(8,128)}, f32[1024,300]{0,1:T(8,128)S(1)}, u32[]{:S(2)}) copy-start(f32[1024,300]{0,1:T(8,128)S(1)} %fusion.3) | copy-start | bytes 3686404
  429.2 1.4 copy-start.2
  433.6 230.8 %all-reduce.12.cloned.1.call-start = ((), (), s32[]{:S(2)}) async-start(), calls=%async_computation.5 | async-start | bytes 933888 | tf_op jit(solution)/shard_map/psum | solution.py:57
  497.6 201.3 %reduce-scatter.2.cloned.1.call-start = ((), (), s32[]{:S(2)}) async-start(), calls=%async_computation.3 | async-start | bytes 1400832 | tf_op jit(solution)/shard_map/reduce_scatter | solution.py:59
Sparse Core Ops, SparseCore 0:
  100.3 63.0 all-reduce.5
  167.2 144.9 all-reduce.7
  433.7 63.7 all-reduce.9
  501.2 145.0 all-reduce.11
  664.5 34.3 reduce-scatter.1
